TPU v7x, 32 devices: a whole 2x2x4 slice. The times are simulated.
32 devices in a mesh: lat: 4 (over y, core), blk: 4 (over z), probe: 2 (over x).
Axes of the slice: x: 2, y: 2, z: 4, core: 2. Of those that a mesh axis runs over, the one named last changes fastest.
Arguments:
- probes_in: bfloat16 [64, 2, 640, 640], P('probe', None, ('lat', 'blk')), may hold values from -1.5 to 1.5
- root_spectrum: float32 [640], replicated, may hold values from 0.2 to 3, as said below
- order_slots: int32 [640], replicated, may hold values from 0 to 639, as said below
- legendre: bfloat16 [640, 640, 1280], P(None, ('lat', 'blk')), as said below
- weight: float32 [1280, 2560], P(('lat', 'blk')), may hold values from 0.2 to 5
- beta: float32 [64], P('probe'), may hold values from 0.5 to 2
Outputs:
- matvec: float32 [64, 2, 640, 640], P('probe', None, ('lat', 'blk'))
- gradient: float32 [1280, 2560], P(('lat', 'blk'), 'probe')
Inputs may be any that keep to these rules, and one draw needn't show every extreme that they name: order_slots is a permutation of 0 to 639, and slots 2k and 2k + 1 hold orders that sum to 639. legendre[l, s, j] is the orthonormal associated Legendre function (no Condon-Shortley sign) of degree l and order order_slots[s] at cos(theta_j), zero for l below the order, rounded to bfloat16. root_spectrum is drawn afresh for each degree.
All inputs are finite; a program needn't handle non-finite values.
Results may differ from a plain program's by a relative error of at most 0.0031.
Values may be sent and summed in bfloat16 or wider, within the bound.
No kernel may reach another device: no remote copies, remote signals or barrier semaphores. Data moves between devices by JAX's collectives and lax.ppermute only.
A program may use at most 320 MiB of HBM per device.

v0:
```python
import functools
import math

import jax
import jax.numpy as jnp
from jax import lax
from jax.experimental import pallas as pl
from jax.experimental.pallas import tpu as pltpu
from jax.sharding import PartitionSpec as P


GROUP = 8
DEPTH = 128
CHUNK = 16
PART = 8
TILE = 256
VMEM_LIMIT = 60 * 2**20


def fourier_tables(orders, lon_count):
    longitude = jnp.arange(lon_count, dtype=jnp.int32)
    phase_idx = orders[:, None] * longitude[None, :] % lon_count
    angle = phase_idx.astype(jnp.float32) * (2.0 * math.pi / lon_count)
    twiddle = jnp.stack([jnp.cos(angle), jnp.sin(angle)])
    upper = twiddle.astype(jnp.bfloat16)
    lower = (twiddle - upper.astype(jnp.float32)).astype(jnp.bfloat16)
    return (upper, lower)


def cycle_work(spectra, inverse_tables, forward_tables, area, weight):
    grid_field = jnp.einsum(
        "pcmj,cmx->pjx", spectra, inverse_tables[0], preferred_element_type=jnp.float32
    )
    grid_field = grid_field + jnp.einsum(
        "pcmj,cmx->pjx", spectra, inverse_tables[1], preferred_element_type=jnp.float32
    )
    squares = grid_field * grid_field
    weighted = (area[None, :, None] * weight[None] * grid_field).astype(jnp.bfloat16)
    analysed = jnp.einsum(
        "pjx,cmx->pcmj", weighted, forward_tables[0], preferred_element_type=jnp.float32
    )
    analysed = analysed + jnp.einsum(
        "pjx,cmx->pcmj", weighted, forward_tables[1], preferred_element_type=jnp.float32
    )
    return (squares, analysed.astype(jnp.bfloat16))


def plain_body(probes_in, root_spectrum, order_slots, legendre, weight, beta):
    groups = lax.axis_size(("lat", "blk"))
    my_index = lax.axis_index(("lat", "blk"))
    cycle_count = weight.shape[0]
    lon_count = weight.shape[1]
    all_cycles = cycle_count * groups
    scaled = (probes_in.astype(jnp.float32) * root_spectrum).astype(jnp.bfloat16)
    spectra = jnp.einsum(
        "pcml,lmj->pcmj", scaled, legendre, preferred_element_type=jnp.float32
    ).astype(jnp.bfloat16)
    cycle_index = (my_index * cycle_count + jnp.arange(cycle_count, dtype=jnp.int32)).astype(
        jnp.float32
    )
    local_sines = jnp.sin(math.pi * (cycle_index + 0.5) / all_cycles)
    area = 2.0 * math.pi / lon_count * (math.pi / all_cycles) * local_sines
    forward_tables = fourier_tables(order_slots, lon_count)
    squares, analysed = cycle_work(
        lax.all_to_all(spectra, ("lat", "blk"), split_axis=3, concat_axis=2, tiled=True),
        forward_tables,
        forward_tables,
        area,
        weight,
    )
    returned = lax.all_to_all(analysed, ("lat", "blk"), split_axis=2, concat_axis=3, tiled=True)
    matvec = (
        jnp.einsum("pcmj,lmj->pcml", returned, legendre, preferred_element_type=jnp.float32)
        * root_spectrum
    )
    grad_terms = jnp.einsum("pjx,p->jx", squares, beta) * area[:, None]
    gradient = lax.psum_scatter(grad_terms, "probe", scatter_dimension=1, tiled=True)
    return (matvec, gradient)


def dot(a, b, dims=((1,), (0,))):
    return lax.dot_general(a, b, (dims, ((), ())), preferred_element_type=jnp.float32)


def split(x):
    upper = x.astype(jnp.bfloat16)
    return upper, (x - upper.astype(jnp.float32)).astype(jnp.bfloat16)


LANES = 128
PITCH = GROUP + 1


def every(slot, count):
    return pl.ds(slot, count, stride=PITCH)


def tiles(ref):
    return range(ref.shape[0])


def put(ref, rows, value):
    for t in tiles(ref):
        ref[t, rows, :] = value[:, t * LANES : (t + 1) * LANES]


def take(ref, rows):
    return jnp.concatenate([ref[t, rows, :] for t in tiles(ref)], axis=-1)


def spread_rows(tbl_ref, wide):
    @pl.loop(0, tbl_ref.shape[0] * 2 // DEPTH)
    def _(step):
        some = pl.ds(step * (DEPTH // 2), DEPTH // 2)
        for t in tiles(wide):
            piece = tbl_ref[some, :, :, t * LANES : (t + 1) * LANES].astype(jnp.float32)
            piece = piece.reshape(DEPTH, GROUP, LANES)
            for i in range(DEPTH):
                wide[t, pl.ds(step * (DEPTH * PITCH) + i * PITCH, GROUP), :] = piece[i]


def table_block(wide, step, slot):
    rows = pl.ds(step * (DEPTH * PITCH) + slot, DEPTH, stride=PITCH)
    return take(wide, rows).astype(jnp.bfloat16)


def slot_signs(orders_ref, base, shape):
    row = lax.broadcasted_iota(jnp.int32, shape, 0)
    odd = jnp.zeros(shape, jnp.int32)
    for slot in range(GROUP):
        odd = jnp.where(row == slot, orders_ref[base + slot] % 2, odd)
    return (1 - 2 * odd).astype(jnp.float32)


def visit(orders_ref, base, turn, pair, steps):
    first = orders_ref[base + 2 * pair] // DEPTH
    mine = turn < steps - first
    slot = 2 * pair + jnp.where(mine, 0, 1)
    return slot, jnp.where(mine, first + turn, turn - 1)


def even_degree(shape):
    return lax.broadcasted_iota(jnp.int32, shape, 1) % 2 == 0


def synth_kernel(orders_ref, me_ref, x_ref, root_ref, tbl_ref, *refs, slots, split_up):
    xs, wide, acc, ns, ss = refs[-6:-1] if split_up else refs[-5:]
    outs = refs[:-6] if split_up else refs[:1]
    out_ref = refs[-1] if split_up else outs[0]
    mine = me_ref[0]
    base = mine * slots + pl.program_id(0) * GROUP
    chunk = x_ref.shape[0]
    cycles = out_ref.shape[3] // chunk
    half = out_ref.shape[0] // 2
    rows = chunk * 2
    scaled = (x_ref[...].astype(jnp.float32) * root_ref[...]).astype(jnp.bfloat16)
    scaled = scaled.astype(jnp.float32).reshape(rows, GROUP, scaled.shape[-1])
    for i in range(rows):
        put(xs, pl.ds(i * PITCH, GROUP), scaled[i])
    acc[...] = jnp.zeros_like(acc)

    spread_rows(tbl_ref, wide)
    steps = tbl_ref.shape[0] * 2 // DEPTH

    @pl.loop(0, steps + 1)
    def _(turn):
        for pair in range(GROUP // 2):
            slot, step = visit(orders_ref, base, turn, pair, steps)
            x = xs[step, every(slot, rows), :]
            even = even_degree(x.shape)
            x = jnp.concatenate([jnp.where(even, x, 0.0), jnp.where(even, 0.0, x)], axis=0)
            table = table_block(wide, step, slot)
            acc[slot] += dot(x.astype(jnp.bfloat16), table)

    for slot in range(GROUP):
        even, odd = acc[slot, :rows], acc[slot, rows:]
        put(ns, every(slot, rows), even + odd)
        put(ss, every(slot, rows), even - odd)
    sign = slot_signs(orders_ref, base, (GROUP, acc.shape[-1]))
    for c in range(2):
        north, south = [], []
        for p in range(chunk):
            place = pl.ds((2 * p + c) * PITCH, GROUP)
            north.append(take(ns, place))
            south.append(take(ss, place) * sign)
        for d in range(half):
            for source, place in ((north, d), (south, 2 * half - 1 - d)):
                pieces = [piece[:, d * cycles : (d + 1) * cycles] for piece in source]
                at = place ^ mine if split_up else place
                out_ref[at, c] = jnp.concatenate(pieces, axis=-1).astype(jnp.bfloat16)
    if split_up:
        for r, out in enumerate(outs):
            out[...] = out_ref[r]


def analysis_kernel(orders_ref, me_ref, root_ref, tbl_ref, *refs, slots, sources, split_up):
    mine = me_ref[0]
    if split_up:
        q_ref = refs[-1]
        refs, parts = refs[:-1], refs[:sources]
        for r, part in enumerate(parts):
            q_ref[mine ^ r] = part[...]
    else:
        q_ref = refs[0]
    out_ref, plus, minus, wide, held, outs = refs[-6:]
    base = mine * slots + pl.program_id(0) * GROUP
    chunk = out_ref.shape[0]
    cycles = q_ref.shape[3] // chunk
    half = q_ref.shape[0] // 2
    rows = chunk * 2

    sign = slot_signs(orders_ref, base, (GROUP, half * cycles))
    for c in range(2):
        blocks = [q_ref[d, c].astype(jnp.float32) for d in range(2 * half)]
        for p in range(chunk):
            cut = slice(p * cycles, (p + 1) * cycles)
            north = jnp.concatenate([blocks[d][:, cut] for d in range(half)], axis=-1)
            other = [blocks[2 * half - 1 - d][:, cut] for d in range(half)]
            south = jnp.concatenate(other, axis=-1) * sign
            place = pl.ds((2 * p + c) * PITCH, GROUP)
            put(plus, place, north + south)
            put(minus, place, north - south)
    for slot in range(GROUP):
        both = [take(ref, every(slot, rows)) for ref in (plus, minus)]
        upper, lower = split(jnp.concatenate(both, axis=0))
        held[slot, : 2 * rows] = upper
        held[slot, 2 * rows :] = lower
    outs[...] = jnp.zeros_like(outs)

    spread_rows(tbl_ref, wide)
    steps = tbl_ref.shape[0] * 2 // DEPTH

    @pl.loop(0, steps + 1)
    def _(turn):
        for pair in range(GROUP // 2):
            slot, step = visit(orders_ref, base, turn, pair, steps)
            now = pl.ds(pl.multiple_of(step * DEPTH, DEPTH), DEPTH)
            table = table_block(wide, step, slot)
            both = dot(held[slot], table, ((1,), (1,)))
            both = both[: 2 * rows] + both[2 * rows :]
            even = even_degree((rows, DEPTH))
            chosen = jnp.where(even, both[:rows], both[rows:])
            outs[step, every(slot, rows), :] = chosen * root_ref[:, now]

    for p in range(chunk):
        for c in range(2):
            out_ref[p, c] = take(outs, pl.ds((2 * p + c) * PITCH, GROUP))


def fourier_kernel(me_ref, *refs, first, sources, split_up):
    ahead_cos, ahead_sin, back_cos, back_sin, w_low, w_high, turn_ref, beta_ref = refs[:8]
    old_low, old_high = (None, None) if first else refs[8:10]
    refs = refs[8:] if first else refs[10:]
    mine_at = me_ref[0]
    step, part = pl.program_id(0), pl.program_id(1)
    if split_up:
        arrived, sent = refs[:sources], refs[sources : 2 * sources]
        g_low, g_high, rc, rs, acc_c, acc_s, middle, r_ref = refs[2 * sources :]

        @pl.when((step == 0) & (part == 0))
        def _():
            for r, piece in enumerate(arrived):
                r_ref[mine_at ^ r] = piece[...]

    else:
        r_ref, out_ref, g_low, g_high, rc, rs, acc_c, acc_s, middle = refs
    slots = r_ref.shape[2]
    tile, lanes = g_low.shape
    count = acc_c.shape[1]
    mine = pl.ds(pl.multiple_of(part * lanes, LANES), lanes)

    @pl.when(step == 0)
    def _():
        for pair in range(sources // 2):
            for c, place in ((0, rc), (1, rs)):
                both = [r_ref[2 * pair + i, c, :, mine].astype(jnp.float32) for i in range(2)]
                place[part, pl.ds(2 * slots * pair, 2 * slots)] = jnp.concatenate(
                    both, axis=0
                ).astype(jnp.bfloat16)
        turned = turn_ref[...] * rc[part].astype(jnp.float32)
        mid = jnp.sum(turned, axis=0, keepdims=True)
        middle[part] = mid
        w_mid = (w_high[pl.ds(0, 1), :] * mid).astype(jnp.bfloat16).astype(jnp.float32)
        acc_c[part] = turn_ref[...] * w_mid
        acc_s[part] = jnp.zeros_like(acc_s[part])

    c_part = dot(ahead_cos[0], rc[part])
    c_part = c_part[:tile] + c_part[tile:]
    s_part = dot(ahead_sin[0], rs[part])
    s_part = s_part[:tile] + s_part[tile:]
    low = c_part + s_part
    row = lax.broadcasted_iota(jnp.int32, low.shape, 0) + step * tile
    high = jnp.where(row == 0, middle[part], c_part - s_part)
    beta = beta_ref[:, mine]
    low_sq = beta * (low * low)
    high_sq = beta * (high * high)

    @pl.when(part == 0)
    def _():
        g_low[...] = low_sq if first else old_low[...] + low_sq
        g_high[...] = high_sq if first else old_high[...] + high_sq

    @pl.when(part > 0)
    def _():
        g_low[...] += low_sq
        g_high[...] += high_sq

    low = (w_low[...] * low).astype(jnp.bfloat16).astype(jnp.float32)
    high = jnp.where(row == 0, 0.0, w_high[...] * high).astype(jnp.bfloat16).astype(jnp.float32)
    for folded, back, acc in ((low + high, back_cos, acc_c), (low - high, back_sin, acc_s)):
        upper, lower = split(folded)
        both = dot(back[...], upper)
        acc[part] += both[:count] + both[count:] + dot(back[pl.ds(0, count), :], lower)

    @pl.when(step == pl.num_programs(0) - 1)
    def _():
        for d in range(sources):
            for c, acc in ((0, acc_c), (1, acc_s)):
                if split_up:
                    start = pl.multiple_of((mine_at ^ d) * slots, GROUP)
                    sent[d][c, :, mine] = acc[part, pl.ds(start, slots)].astype(jnp.bfloat16)
                else:
                    found = acc[part, pl.ds(slots * d, slots)]
                    out_ref[d, c, :, mine] = found.astype(jnp.bfloat16)


def half_tables(orders, lon_count):
    half = lon_count // 2

    def trig(points):
        idx = orders[:, None] * points[None, :] % lon_count
        angle = idx.astype(jnp.float32) * (2.0 * math.pi / lon_count)
        return lax.optimization_barrier((jnp.cos(angle), jnp.sin(angle)))

    def joined(parts, shape, axes):
        (ca, sa), (cb, sb) = parts
        ca, sa = (t[axes[0]] for t in (ca, sa))
        cb, sb = (t[axes[1]] for t in (cb, sb))
        cosine = (ca * cb - sa * sb).reshape(shape)
        sine = (sa * cb + ca * sb).reshape(shape)
        return split(cosine) + split(sine)

    count = orders.shape[0]
    fine = 128
    coarse_points = jnp.arange(half // fine, dtype=jnp.int32) * fine
    fine_points = jnp.arange(fine, dtype=jnp.int32)
    coarse, small = trig(coarse_points), trig(fine_points)
    every = slice(None)
    back = joined((coarse, small), (count, half), ((every, every, None), (every, None, every)))
    coarse_t = tuple(t.T for t in coarse)
    small_t = tuple(t.T for t in small)
    ahead = joined((coarse_t, small_t), (half, count), ((every, None, every), (None, every, every)))
    tiled = [t.reshape(half // TILE, TILE, count) for t in ahead]
    ahead = [jnp.concatenate(tiled[i : i + 2], axis=1) for i in (0, 2)]
    back = [jnp.concatenate(back[i : i + 2], axis=0) for i in (0, 2)]
    return ahead, back


def fast_body(probes_in, root_spectrum, order_slots, legendre, weight, beta):
    axes = ("lat", "blk")
    groups = lax.axis_size(axes)
    my_index = lax.axis_index(axes)
    cycles, lon_count = weight.shape
    half_lon = lon_count // 2
    all_cycles = cycles * groups
    half_cycles = all_cycles // 2
    degrees, slots = legendre.shape[:2]
    orders_count = order_slots.shape[0]
    probes = probes_in.shape[0]
    chunks = probes // CHUNK
    lanes = CHUNK * cycles
    part_lanes = PART * cycles
    parts = CHUNK // PART
    south = my_index >= groups // 2
    params = functools.partial(pltpu.CompilerParams, vmem_limit_bytes=VMEM_LIMIT)
    f32, bf16 = jnp.float32, jnp.bfloat16

    me = my_index[None].astype(jnp.int32)
    root = root_spectrum[None, :]
    table = legendre.reshape(degrees // 2, 2, slots, all_cycles)
    rows = CHUNK * 2
    whole = lambda shape: pl.BlockSpec(shape, lambda *_: (0,) * len(shape))
    table_spec = pl.BlockSpec((degrees // 2, 2, GROUP, half_cycles), lambda g, *_: (0, 0, g, 0))
    payload_spec = pl.BlockSpec((groups, 2, GROUP, lanes), lambda g, *_: (0, 0, g, 0))
    payload = jax.ShapeDtypeStruct((groups, 2, slots, lanes), bf16)
    table_bytes = degrees * slots * half_cycles * 2
    legendre_cost = pl.CostEstimate(
        flops=1000 * table_bytes, bytes_accessed=table_bytes, transcendentals=0
    )
    tiled = lambda width, height: pltpu.VMEM((width // LANES, height, LANES), f32)
    degree_tiles = tiled(degrees, rows * PITCH)
    cycle_tiles = tiled(half_cycles, rows * PITCH)
    wide = tiled(half_cycles, degrees * PITCH)

    def chunk_spec(q):
        return pl.BlockSpec((CHUNK, 2, GROUP, degrees), lambda g, *_: (q, 0, g, 0))

    piece = jax.ShapeDtypeStruct((2, slots, lanes), bf16)
    piece_spec = pl.BlockSpec((2, GROUP, lanes), lambda g, *_: (0, g, 0))
    stack = pltpu.VMEM((groups, 2, GROUP, lanes), bf16)

    def synth(q, split_up):
        return pl.pallas_call(
            functools.partial(synth_kernel, slots=slots, split_up=split_up),
            name="synth",
            grid_spec=pltpu.PrefetchScalarGridSpec(
                num_scalar_prefetch=2,
                grid=(slots // GROUP,),
                in_specs=[chunk_spec(q), whole(root.shape), table_spec],
                out_specs=[piece_spec] * groups if split_up else payload_spec,
                scratch_shapes=[
                    degree_tiles,
                    wide,
                    pltpu.VMEM((GROUP, 2 * rows, half_cycles), f32),
                    cycle_tiles,
                    cycle_tiles,
                ]
                + ([stack] if split_up else []),
            ),
            out_shape=[piece] * groups if split_up else payload,
            compiler_params=params(),
            cost_estimate=legendre_cost,
        )(order_slots, me, probes_in, root, table)

    def analyse(q, returned, held, split_up):
        first = held is None
        arrays = list(returned) if split_up else [returned]
        return pl.pallas_call(
            functools.partial(
                analysis_kernel, slots=slots, sources=groups, split_up=split_up
            ),
            name="analyse",
            grid_spec=pltpu.PrefetchScalarGridSpec(
                num_scalar_prefetch=2,
                grid=(slots // GROUP,),
                in_specs=[whole(root.shape), table_spec]
                + [piece_spec if split_up else payload_spec] * len(arrays)
                + ([] if first else [pl.BlockSpec(memory_space=pl.ANY)]),
                out_specs=chunk_spec(q),
                scratch_shapes=[
                    cycle_tiles,
                    cycle_tiles,
                    wide,
                    pltpu.VMEM((GROUP, 4 * rows, half_cycles), bf16),
                    degree_tiles,
                ]
                + ([stack] if split_up else []),
            ),
            out_shape=jax.ShapeDtypeStruct((probes, 2, slots, degrees), f32),
            input_output_aliases={} if first else {4 + len(arrays): 0},
            compiler_params=params(),
            cost_estimate=legendre_cost,
        )(order_slots, me, root, table, *arrays, *([] if first else [held]))

    ahead_spec = pl.BlockSpec((1, 2 * TILE, orders_count), lambda i, h, o: (i, 0, 0))
    back_spec = pl.BlockSpec((2 * orders_count, TILE), lambda i, h, o: (0, i))
    grid_spec = pl.BlockSpec((TILE, part_lanes), lambda i, h, o: (i, 0))

    def fourier(received, tables, w_low, w_high, turn, chunk_beta, old, split_up):
        first = old is None
        ahead, back = tables
        square = jax.ShapeDtypeStruct((half_lon, part_lanes), f32)
        arrays = list(received) if split_up else [received]
        shapes = [piece] * groups if split_up else [payload]
        specs = [whole(shape.shape) for shape in shapes]
        return pl.pallas_call(
            functools.partial(
                fourier_kernel, first=first, sources=groups, split_up=split_up
            ),
            name="fourier",
            grid_spec=pltpu.PrefetchScalarGridSpec(
                num_scalar_prefetch=1,
                grid=(half_lon // TILE, parts),
                in_specs=[ahead_spec] * 2
                + [back_spec] * 2
                + [grid_spec] * 2
                + [whole((orders_count, 1)), whole((1, lanes))]
                + ([] if first else [grid_spec] * 2)
                + specs,
                out_specs=specs + [grid_spec, grid_spec],
                scratch_shapes=[pltpu.VMEM((parts, orders_count, part_lanes), bf16)] * 2
                + [pltpu.VMEM((parts, orders_count, part_lanes), f32)] * 2
                + [pltpu.VMEM((parts, 1, part_lanes), f32)]
                + ([pltpu.VMEM(payload.shape, bf16)] if split_up else []),
            ),
            out_shape=shapes + [square, square],
            input_output_aliases={} if first else {9: len(shapes), 10: len(shapes) + 1},
            compiler_params=params(),
            cost_estimate=pl.CostEstimate(
                flops=40 * half_lon * lanes * orders_count,
                bytes_accessed=16 * half_lon * orders_count + 16 * half_lon * part_lanes,
                transcendentals=0,
            ),
        )(
            me,
            *ahead,
            *back,
            w_low,
            w_high,
            turn,
            chunk_beta,
            *([] if first else old),
            *arrays,
        )

    def exchange(x, split_up):
        if split_up:
            pieces = [x[0]]
            for r in range(1, groups):
                pairs = [(i, i ^ r) for i in range(groups)]
                pieces.append(lax.ppermute(x[r], axes, pairs))
            return pieces
        return lax.all_to_all(x, axes, split_axis=0, concat_axis=0, tiled=True)

    local = jnp.arange(cycles, dtype=jnp.int32)
    flipped = jnp.where(south, cycles - 1 - local, local)
    cycle_index = (my_index * cycles + flipped).astype(f32)
    area = 2.0 * math.pi / lon_count * (math.pi / all_cycles) * jnp.sin(
        math.pi * (cycle_index + 0.5) / all_cycles
    )
    turned = jnp.where(south, jnp.flip(weight, 0), weight)
    turned = (area[:, None] * turned).T
    w_low = jnp.tile(turned[:half_lon], (1, PART))
    w_high = jnp.concatenate(
        [turned[half_lon : half_lon + 1], jnp.flip(turned[half_lon + 1 :], 0)], axis=0
    )
    w_high = jnp.tile(w_high, (1, PART))
    turn = (1 - 2 * (order_slots % 2)).astype(f32)[:, None]
    tables = half_tables(order_slots, lon_count)

    split_up = [q % 2 == 1 for q in range(chunks)]
    received = [exchange(synth(q, split_up[q]), split_up[q]) for q in range(chunks)]
    old, held = None, None
    returned = []
    for q in range(chunks):
        chunk_beta = jnp.repeat(beta[q * CHUNK : (q + 1) * CHUNK], cycles)[None, :]
        *analysed, low, high = fourier(
            received[q], tables, w_low, w_high, turn, chunk_beta, old, split_up[q]
        )
        old = (low, high)
        ready = analysed if split_up[q] else analysed[0]
        returned.append(exchange(ready, split_up[q]))
    for q in range(chunks):
        held = analyse(q, returned[q], held, split_up[q])

    lane_cycle = jnp.arange(part_lanes, dtype=jnp.int32) % cycles
    pick = (lane_cycle[None, :] == flipped[:, None]).astype(f32)
    sums = [
        lax.dot_general(
            pick, s, (((1,), (1,)), ((), ())), precision=lax.Precision.HIGHEST,
            preferred_element_type=f32,
        )
        for s in old
    ]
    natural = 2.0 * math.pi / lon_count * (math.pi / all_cycles) * jnp.sin(
        math.pi * ((my_index * cycles + local).astype(f32) + 0.5) / all_cycles
    )
    if lax.axis_size("probe") == 2:
        ahead_half = lax.axis_index("probe") == 0
        keep = jnp.where(ahead_half, sums[0], sums[1])
        give = jnp.where(ahead_half, sums[1], sums[0])
        half = (keep + lax.ppermute(give, "probe", [(0, 1), (1, 0)])) * natural[:, None]
        mirrored = jnp.concatenate([half[:, :1], jnp.flip(half[:, 1:], 1)], axis=1)
        gradient = jnp.where(ahead_half, half, mirrored)
    else:
        terms = jnp.concatenate([sums[0], sums[1][:, :1], jnp.flip(sums[1][:, 1:], 1)], axis=1)
        gradient = lax.psum_scatter(
            terms * natural[:, None], "probe", scatter_dimension=1, tiled=True
        )
    return (held, gradient)


def body(probes_in, root_spectrum, order_slots, legendre, weight, beta):
    degrees, slots, all_cycles = legendre.shape
    fits = (
        slots % GROUP == 0
        and degrees % DEPTH == 0
        and degrees == order_slots.shape[0]
        and all_cycles % (2 * LANES) == 0
        and (PART * weight.shape[0]) % LANES == 0
        and probes_in.shape[0] % CHUNK == 0
        and weight.shape[1] % (2 * TILE) == 0
        and lax.axis_size(("lat", "blk")) in (2, 4, 8, 16, 32)
    )
    chosen = fast_body if fits else plain_body
    return chosen(probes_in, root_spectrum, order_slots, legendre, weight, beta)


def solution(mesh):
    return jax.shard_map(
        body,
        mesh=mesh,
        in_specs=(
            P("probe", None, ("lat", "blk"), None),
            P(),
            P(),
            P(None, ("lat", "blk"), None),
            P(("lat", "blk"), None),
            P("probe"),
        ),
        out_specs=(P("probe", None, ("lat", "blk"), None), P(("lat", "blk"), "probe")),
        check_vma=False,
    )
```

profile of v0, /device:TPU:0, one launch (start us, length us, event | category | flops | bytes accessed | tf_op | source)
XLA Modules:
  0.0 432.9 jit_solution(2743307416774470184)
XLA Ops:
  1.9 20.4 %synth.2 = bf16[16,2,40,1280]{3,2,1,0:T(8,128)(2,1)} custom-call(s32[640]{0:T(1024)} %orders_ref.7, s32[1]{0:T(128)} %bitcast.me_ref, bf16[32,2,40,640]{3,2,1,0:T(8,128)(2,1)} %x_ref.3, f32[1,640]{1,0:T(1,128)} %broadcast_in_dim.11.root_ref, bf16[320,2,40,1280]{3,2,1,0:T(8,128)(2,1)} %bitcast.41), custom_call_target="tpu_custom_call" | custom-call | flops 32768000000 | bytes 32768000 | tf_op jit(solution)/shard_map/synth/pallas_call | solution.py:403
  22.3 7.5 %all-to-all-start = ((bf16[16,2,40,1280]{3,2,1,0:T(8,128)(2,1)}), bf16[16,2,40,1280]{3,2,1,0:T(8,128)(2,1)}, u32[]{:S(2)}, u32[]{:S(2)}) async-start(bf16[16,2,40,1280]{3,2,1,0:T(8,128)(2,1)} %synth.2), calls=%async_computation | async-start | bytes 6553600 | tf_op jit(solution)/shard_map/all_to_all | solution.py:513
  29.8 20.7 %synth.3 = (bf16[2,40,1280]{2,1,0:T(8,128)(2,1)}, bf16[2,40,1280]{2,1,0:T(8,128)(2,1)}, bf16[2,40,1280]{2,1,0:T(8,128)(2,1)}, bf16[2,40,1280]{2,1,0:T(8,128)(2,1...) custom-call(s32[640]{0:T(1024)} %orders_ref.7, ...), custom_call_target="tpu_custom_call" | custom-call | flops 32768000000 | bytes 32768000 | tf_op jit(solution)/shard_map/synth/pallas_call | solution.py:403
  63.9 4.6 %copy.19 = f32[640,1280]{1,0:T(8,128)} copy(f32[640,1280]{0,1:T(8,128)} %bitcast.32) | data formatting | bytes 6553600 | tf_op jit(solution)/shard_map/add | solution.py:340
  68.5 2.9 copy.17
  71.4 4.4 %reverse = f32[1280,80]{0,1:T(8,128)S(1)} reverse(f32[1280,80]{0,1:T(8,128)} %bitcast.37), dimensions={0} | reverse | bytes 819200
  78.2 2.9 fusion
  83.3 3.1 pad_maximum_fusion.2
  89.6 3.2 copy.25.refs_5_
  94.0 3.2 copy.24.refs_4_
  98.8 4.0 pad_maximum_fusion.refs_0_
  102.9 2.7 collective-permute-start.13
  105.6 16.6 %collective-permute-done.1.refs_12_ = bf16[2,40,1280]{2,1,0:T(8,128)(2,1)} collective-permute-done((bf16[2,40,1280]{2,1,0:T(8,128)(2,1)}, bf16[2,40,1280]{2,1,0:T(8,128)(2,1)}, u32[]{:S(2)}, u32[]{:S(2)}) %collective-permute-start.1) | collective-permute-done | bytes 204832 | tf_op jit(solution)/shard_map/ppermute | solution.py:511
  122.2 4.3 collective-permute-start.14
  127.1 4.0 collective-permute-start.4
  131.1 40.4 %fourier.2 = (bf16[16,2,40,1280]{3,2,1,0:T(8,128)(2,1)}, f32[1280,640]{1,0:T(8,128)}, f32[1280,640]{1,0:T(8,128)}) custom-call(s32[1]{0:T(128)} %bitcast.me_ref, bf16[5,512,640]{2,1,0:T(8,128)(2,1)} %pad_maximum_fusion.refs_0_, bf16[5,512,640]{2,1,0:T(8,128)(2,1)} %pad_maximum_fusion.1.refs_1_, bf16[1280,1280]{1,0:T(8,128)(2,1)} %get-tuple-element.106.refs_2_, ...), custom_call_target="tpu_custom_call" | custom-call | flops 41943040000 | bytes 26214400 | tf_op jit(solution)/shard_map/fourier/pallas_call | solution.py:466
  171.5 4.6 %all-to-all-start.1 = ((bf16[16,2,40,1280]{3,2,1,0:T(8,128)(2,1)}), bf16[16,2,40,1280]{3,2,1,0:T(8,128)(2,1)}, u32[]{:S(2)}, u32[]{:S(2)}) async-start(bf16[16,2,40,1280]{3,2,1,0:T(8,128)(2,1)} %get-tuple-element.81), calls=%async_computation.1 | async-start | bytes 6553600 | tf_op jit(solution)/shard_map/all_to_all | solution.py:513
  181.9 3.9 collective-permute-start.9
  186.5 82.4 %collective-permute-done.5.refs_16_ = bf16[2,40,1280]{2,1,0:T(8,128)(2,1)S(1)} collective-permute-done((bf16[2,40,1280]{2,1,0:T(8,128)(2,1)S(1)}, bf16[2,40,1280]{2,1,0:T(8,128)(2,1)S(1)}, u32[]{:S(2)}, u32[]{:S(2)}) %collective-permute-start.5) | collective-permute-done | bytes 204832 | tf_op jit(solution)/shard_map/ppermute | solution.py:511
  269.0 10.4 %collective-permute-done.9.refs_20_ = bf16[2,40,1280]{2,1,0:T(8,128)(2,1)S(1)} collective-permute-done((bf16[2,40,1280]{2,1,0:T(8,128)(2,1)S(1)}, bf16[2,40,1280]{2,1,0:T(8,128)(2,1)S(1)}, u32[]{:S(2)}, u32[]{:S(2)}) %collective-permute-start.9) | collective-permute-done | bytes 204832 | tf_op jit(solution)/shard_map/ppermute | solution.py:511
  280.0 41.8 %fourier.3 = (bf16[2,40,1280]{2,1,0:T(8,128)(2,1)}, bf16[2,40,1280]{2,1,0:T(8,128)(2,1)}, bf16[2,40,1280]{2,1,0:T(8,128)(2,1)}, bf16[2,40,1280]{2,1,0:T(8,128)(2...) custom-call(s32[1]{0:T(128)} %bitcast.me_ref, ...), custom_call_target="tpu_custom_call", output_to_operand_aliasing={{16}: (9, {}), {17}: (10, {})} | custom-call | flops 41943040000 | bytes 26214400 | tf_op jit(solution)/shard_map/fourier/pallas_call | solution.py:466
  321.8 3.8 fusion.11
  329.1 2.7 collective-permute-start.16
  333.5 5.0 %collective-permute-done.30 = f32[80,1280]{1,0:T(8,128)S(1)} collective-permute-done((f32[80,1280]{1,0:T(8,128)S(1)}, f32[80,1280]{1,0:T(8,128)S(1)}, u32[]{:S(2)}, u32[]{:S(2)}) %collective-permute-start.30) | collective-permute-done | bytes 409632 | tf_op jit(solution)/shard_map/ppermute | solution.py:562
  339.8 3.0 collective-permute-start.20
  342.8 4.3 collective-permute-done.16.refs_2_
  347.6 14.7 %collective-permute-start.23 = (bf16[2,40,1280]{2,1,0:T(8,128)(2,1)S(1)}, bf16[2,40,1280]{2,1,0:T(8,128)(2,1)S(1)}, u32[]{:S(2)}, u32[]{:S(2)}) collective-permute-start(bf16[2,40,1280]{2,1,0:T(8,128)(2,1)S(1)} %copy-done.27), channel_id=1, source_target_pairs={{0,18},{2,16},{4,22},{6,20},{8,26},{10,24},{12,30},{14,28},{16,2},... | collective-permute-start | bytes 614408 | tf_op jit(solution)/shard_map/ppermute | solution.py:511
  365.6 4.4 %collective-permute-start.26 = (bf16[2,40,1280]{2,1,0:T(8,128)(2,1)S(1)}, bf16[2,40,1280]{2,1,0:T(8,128)(2,1)S(1)}, u32[]{:S(2)}, u32[]{:S(2)}) collective-permute-start(bf16[2,40,1280]{2,1,0:T(8,128)(2,1)S(1)} %copy-done.23), channel_id=1, source_target_pairs={{0,24},{2,26},{4,28},{6,30},{8,16},{10,18},{12,20},{14,22},{16,8},... | collective-permute-start | bytes 614408 | tf_op jit(solution)/shard_map/ppermute | solution.py:511
  370.0 8.5 %collective-permute-start.27 = (bf16[2,40,1280]{2,1,0:T(8,128)(2,1)S(1)}, bf16[2,40,1280]{2,1,0:T(8,128)(2,1)S(1)}, u32[]{:S(2)}, u32[]{:S(2)}) collective-permute-start(bf16[2,40,1280]{2,1,0:T(8,128)(2,1)S(1)} %copy-done.22), channel_id=1, source_target_pairs={{0,26},{2,24},{4,30},{6,28},{8,18},{10,16},{12,22},{14,20},{16,10}... | collective-permute-start | bytes 614408 | tf_op jit(solution)/shard_map/ppermute | solution.py:511
  378.8 3.2 collective-permute-done.24.refs_10_
  383.4 23.8 %analyse.2.refs_16_ = f32[32,2,40,640]{3,2,1,0:T(8,128)} custom-call(s32[640]{0:T(1024)} %orders_ref.7, s32[1]{0:T(128)} %bitcast.me_ref, f32[1,640]{1,0:T(1,128)} %broadcast_in_dim.11.root_ref, bf16[320,2,40,1280]{3,2,1,0:T(8,128)(2,1)} %bitcast.43, bf16[16,2,40,1280]{3,2,1,0:T(8,128)(2,1)} %all-to-all-done.1.refs_0_), custom_call_target="tpu_custom_call" | custom-call | flops 32768000000 | bytes 32768000 | tf_op jit(solution)/shard_map/analyse/pallas_call | solution.py:428
  408.3 24.4 %analyse.3 = f32[32,2,40,640]{3,2,1,0:T(8,128)} custom-call(s32[640]{0:T(1024)} %orders_ref.7, s32[1]{0:T(128)} %bitcast.me_ref, f32[1,640]{1,0:T(1,128)} %broadcast_in_dim.11.root_ref, bf16[320,2,40,1280]{3,2,1,0:T(8,128)(2,1)} %bitcast.44, bf16[2,40,1280]{2,1,0:T(8,128)(2,1)} %get-tuple-element.65.refs_0_, ...), custom_call_target="tpu_custom_call", output_to_operand_aliasing={{}: (20, {})} | custom-call | flops 32768000000 | bytes 32768000 | tf_op jit(solution)/shard_map/analyse/pallas_call | solution.py:428
  (188 shorter events, 45.7 us)
Async XLA Ops:
  22.3 108.8 %all-to-all-start = ((bf16[16,2,40,1280]{3,2,1,0:T(8,128)(2,1)}), bf16[16,2,40,1280]{3,2,1,0:T(8,128)(2,1)}, u32[]{:S(2)}, u32[]{:S(2)}) async-start(bf16[16,2,40,1280]{3,2,1,0:T(8,128)(2,1)} %synth.2), calls=%async_computation | async-start | bytes 6553600 | tf_op jit(solution)/shard_map/all_to_all | solution.py:513
  50.5 52.4 %collective-permute-start = (bf16[2,40,1280]{2,1,0:T(8,128)(2,1)}, bf16[2,40,1280]{2,1,0:T(8,128)(2,1)}, u32[]{:S(2)}, u32[]{:S(2)}) collective-permute-start(bf16[2,40,1280]{2,1,0:T(8,128)(2,1)} %get-tuple-element.50), channel_id=1, source_target_pairs={{0,2},{2,0},{4,6},{6,4},{8,10},{10,8},{12,14},{14,12},{16,18},{18,... | collective-permute-start | bytes 614408 | tf_op jit(solution)/shard_map/ppermute | solution.py:511
  52.4 69.8 %collective-permute-start.1 = (bf16[2,40,1280]{2,1,0:T(8,128)(2,1)}, bf16[2,40,1280]{2,1,0:T(8,128)(2,1)}, u32[]{:S(2)}, u32[]{:S(2)}) collective-permute-start(bf16[2,40,1280]{2,1,0:T(8,128)(2,1)} %get-tuple-element.51), channel_id=1, source_target_pairs={{0,4},{2,6},{4,0},{6,2},{8,12},{10,14},{12,8},{14,10},{16,20},{18,... | collective-permute-start | bytes 614408 | tf_op jit(solution)/shard_map/ppermute | solution.py:511
  54.8 71.7 %collective-permute-start.10 = (bf16[2,40,1280]{2,1,0:T(8,128)(2,1)}, bf16[2,40,1280]{2,1,0:T(8,128)(2,1)}, u32[]{:S(2)}, u32[]{:S(2)}) collective-permute-start(bf16[2,40,1280]{2,1,0:T(8,128)(2,1)} %get-tuple-element.60), channel_id=1, source_target_pairs={{0,22},{2,20},{4,18},{6,16},{8,30},{10,28},{12,26},{14,24},{16,6},... | collective-permute-start | bytes 614408 | tf_op jit(solution)/shard_map/ppermute | solution.py:511
  56.2 70.3 %collective-permute-start.11 = (bf16[2,40,1280]{2,1,0:T(8,128)(2,1)}, bf16[2,40,1280]{2,1,0:T(8,128)(2,1)}, u32[]{:S(2)}, u32[]{:S(2)}) collective-permute-start(bf16[2,40,1280]{2,1,0:T(8,128)(2,1)} %get-tuple-element.61), channel_id=1, source_target_pairs={{0,24},{2,26},{4,28},{6,30},{8,16},{10,18},{12,20},{14,22},{16,8},... | collective-permute-start | bytes 614408 | tf_op jit(solution)/shard_map/ppermute | solution.py:511
  56.2 70.9 %collective-permute-start.12 = (bf16[2,40,1280]{2,1,0:T(8,128)(2,1)}, bf16[2,40,1280]{2,1,0:T(8,128)(2,1)}, u32[]{:S(2)}, u32[]{:S(2)}) collective-permute-start(bf16[2,40,1280]{2,1,0:T(8,128)(2,1)} %get-tuple-element.62), channel_id=1, source_target_pairs={{0,26},{2,24},{4,30},{6,28},{8,18},{10,16},{12,22},{14,20},{16,10}... | collective-permute-start | bytes 614408 | tf_op jit(solution)/shard_map/ppermute | solution.py:511
  102.9 73.3 %collective-permute-start.13 = (bf16[2,40,1280]{2,1,0:T(8,128)(2,1)S(1)}, bf16[2,40,1280]{2,1,0:T(8,128)(2,1)S(1)}, u32[]{:S(2)}, u32[]{:S(2)}) collective-permute-start(bf16[2,40,1280]{2,1,0:T(8,128)(2,1)S(1)} %copy-done.20), channel_id=1, source_target_pairs={{0,28},{2,30},{4,24},{6,26},{8,20},{10,22},{12,16},{14,18},{16,12}... | collective-permute-start | bytes 614408 | tf_op jit(solution)/shard_map/ppermute | solution.py:511
  122.2 56.5 %collective-permute-start.14 = (bf16[2,40,1280]{2,1,0:T(8,128)(2,1)S(1)}, bf16[2,40,1280]{2,1,0:T(8,128)(2,1)S(1)}, u32[]{:S(2)}, u32[]{:S(2)}) collective-permute-start(bf16[2,40,1280]{2,1,0:T(8,128)(2,1)S(1)} %copy-done.18), channel_id=1, source_target_pairs={{0,30},{2,28},{4,26},{6,24},{8,22},{10,20},{12,18},{14,16},{16,14}... | collective-permute-start | bytes 614408 | tf_op jit(solution)/shard_map/ppermute | solution.py:511
  126.5 53.7 %collective-permute-start.2 = (bf16[2,40,1280]{2,1,0:T(8,128)(2,1)S(1)}, bf16[2,40,1280]{2,1,0:T(8,128)(2,1)S(1)}, u32[]{:S(2)}, u32[]{:S(2)}) collective-permute-start(bf16[2,40,1280]{2,1,0:T(8,128)(2,1)S(1)} %copy-done.17), channel_id=1, source_target_pairs={{0,6},{2,4},{4,2},{6,0},{8,14},{10,12},{12,10},{14,8},{16,22},{18,... | collective-permute-start | bytes 614408 | tf_op jit(solution)/shard_map/ppermute | solution.py:511
  126.5 55.2 %collective-permute-start.3 = (bf16[2,40,1280]{2,1,0:T(8,128)(2,1)S(1)}, bf16[2,40,1280]{2,1,0:T(8,128)(2,1)S(1)}, u32[]{:S(2)}, u32[]{:S(2)}) collective-permute-start(bf16[2,40,1280]{2,1,0:T(8,128)(2,1)S(1)} %copy-done.16), channel_id=1, source_target_pairs={{0,8},{2,10},{4,12},{6,14},{8,0},{10,2},{12,4},{14,6},{16,24},{18,... | collective-permute-start | bytes 614408 | tf_op jit(solution)/shard_map/ppermute | solution.py:511
  127.1 54.8 %collective-permute-start.4 = (bf16[2,40,1280]{2,1,0:T(8,128)(2,1)S(1)}, bf16[2,40,1280]{2,1,0:T(8,128)(2,1)S(1)}, u32[]{:S(2)}, u32[]{:S(2)}) collective-permute-start(bf16[2,40,1280]{2,1,0:T(8,128)(2,1)S(1)} %copy-done.15), channel_id=1, source_target_pairs={{0,10},{2,8},{4,14},{6,12},{8,2},{10,0},{12,6},{14,4},{16,26},{18,... | collective-permute-start | bytes 614408 | tf_op jit(solution)/shard_map/ppermute | solution.py:511
  171.5 211.9 %all-to-all-start.1 = ((bf16[16,2,40,1280]{3,2,1,0:T(8,128)(2,1)}), bf16[16,2,40,1280]{3,2,1,0:T(8,128)(2,1)}, u32[]{:S(2)}, u32[]{:S(2)}) async-start(bf16[16,2,40,1280]{3,2,1,0:T(8,128)(2,1)} %get-tuple-element.81), calls=%async_computation.1 | async-start | bytes 6553600 | tf_op jit(solution)/shard_map/all_to_all | solution.py:513
  176.2 92.7 %collective-permute-start.5 = (bf16[2,40,1280]{2,1,0:T(8,128)(2,1)S(1)}, bf16[2,40,1280]{2,1,0:T(8,128)(2,1)S(1)}, u32[]{:S(2)}, u32[]{:S(2)}) collective-permute-start(bf16[2,40,1280]{2,1,0:T(8,128)(2,1)S(1)} %copy-done.14), channel_id=1, source_target_pairs={{0,12},{2,14},{4,8},{6,10},{8,4},{10,6},{12,0},{14,2},{16,28},{18,... | collective-permute-start | bytes 614408 | tf_op jit(solution)/shard_map/ppermute | solution.py:511
  178.7 90.2 %collective-permute-start.6 = (bf16[2,40,1280]{2,1,0:T(8,128)(2,1)S(1)}, bf16[2,40,1280]{2,1,0:T(8,128)(2,1)S(1)}, u32[]{:S(2)}, u32[]{:S(2)}) collective-permute-start(bf16[2,40,1280]{2,1,0:T(8,128)(2,1)S(1)} %copy-done.13), channel_id=1, source_target_pairs={{0,14},{2,12},{4,10},{6,8},{8,6},{10,4},{12,2},{14,0},{16,30},{18,... | collective-permute-start | bytes 614408 | tf_op jit(solution)/shard_map/ppermute | solution.py:511
  180.2 88.7 %collective-permute-start.7 = (bf16[2,40,1280]{2,1,0:T(8,128)(2,1)S(1)}, bf16[2,40,1280]{2,1,0:T(8,128)(2,1)S(1)}, u32[]{:S(2)}, u32[]{:S(2)}) collective-permute-start(bf16[2,40,1280]{2,1,0:T(8,128)(2,1)S(1)} %copy-done.12), channel_id=1, source_target_pairs={{0,16},{2,18},{4,20},{6,22},{8,24},{10,26},{12,28},{14,30},{16,0},... | collective-permute-start | bytes 614408 | tf_op jit(solution)/shard_map/ppermute | solution.py:511
  181.8 87.2 %collective-permute-start.8 = (bf16[2,40,1280]{2,1,0:T(8,128)(2,1)S(1)}, bf16[2,40,1280]{2,1,0:T(8,128)(2,1)S(1)}, u32[]{:S(2)}, u32[]{:S(2)}) collective-permute-start(bf16[2,40,1280]{2,1,0:T(8,128)(2,1)S(1)} %copy-done.11), channel_id=1, source_target_pairs={{0,18},{2,16},{4,22},{6,20},{8,26},{10,24},{12,30},{14,28},{16,2},... | collective-permute-start | bytes 614408 | tf_op jit(solution)/shard_map/ppermute | solution.py:511
  181.9 97.4 %collective-permute-start.9 = (bf16[2,40,1280]{2,1,0:T(8,128)(2,1)S(1)}, bf16[2,40,1280]{2,1,0:T(8,128)(2,1)S(1)}, u32[]{:S(2)}, u32[]{:S(2)}) collective-permute-start(bf16[2,40,1280]{2,1,0:T(8,128)(2,1)S(1)} %copy-done.10), channel_id=1, source_target_pairs={{0,20},{2,22},{4,16},{6,18},{8,28},{10,30},{12,24},{14,26},{16,4},... | collective-permute-start | bytes 614408 | tf_op jit(solution)/shard_map/ppermute | solution.py:511
  327.5 11.0 %collective-permute-start.30 = (f32[80,1280]{1,0:T(8,128)S(1)}, f32[80,1280]{1,0:T(8,128)S(1)}, u32[]{:S(2)}, u32[]{:S(2)}) collective-permute-start(f32[80,1280]{1,0:T(8,128)S(1)} %get-tuple-element.102), channel_id=1, source_target_pairs={{0,1},{1,0},{2,3},{3,2},{4,5},{5,4},{6,7},{7,6},{8,9},{9,8},{10,11... | collective-permute-start | bytes 1228808 | tf_op jit(solution)/shard_map/ppermute | solution.py:562
  329.1 17.9 %collective-permute-start.16 = (bf16[2,40,1280]{2,1,0:T(8,128)(2,1)}, bf16[2,40,1280]{2,1,0:T(8,128)(2,1)S(1)}, u32[]{:S(2)}, u32[]{:S(2)}) collective-permute-start(bf16[2,40,1280]{2,1,0:T(8,128)(2,1)} %get-tuple-element.67), channel_id=1, source_target_pairs={{0,4},{2,6},{4,0},{6,2},{8,12},{10,14},{12,8},{14,10},{16,20},{18,... | collective-permute-start | bytes 614408 | tf_op jit(solution)/shard_map/ppermute | solution.py:511
  331.8 15.2 %collective-permute-start.17 = (bf16[2,40,1280]{2,1,0:T(8,128)(2,1)}, bf16[2,40,1280]{2,1,0:T(8,128)(2,1)S(1)}, u32[]{:S(2)}, u32[]{:S(2)}) collective-permute-start(bf16[2,40,1280]{2,1,0:T(8,128)(2,1)} %get-tuple-element.68), channel_id=1, source_target_pairs={{0,6},{2,4},{4,2},{6,0},{8,14},{10,12},{12,10},{14,8},{16,22},{18,... | collective-permute-start | bytes 614408 | tf_op jit(solution)/shard_map/ppermute | solution.py:511
  333.5 14.1 %collective-permute-start.18 = (bf16[2,40,1280]{2,1,0:T(8,128)(2,1)}, bf16[2,40,1280]{2,1,0:T(8,128)(2,1)}, u32[]{:S(2)}, u32[]{:S(2)}) collective-permute-start(bf16[2,40,1280]{2,1,0:T(8,128)(2,1)} %get-tuple-element.69), channel_id=1, source_target_pairs={{0,8},{2,10},{4,12},{6,14},{8,0},{10,2},{12,4},{14,6},{16,24},{18,... | collective-permute-start | bytes 614408 | tf_op jit(solution)/shard_map/ppermute | solution.py:511
  338.5 23.8 %collective-permute-start.19 = (bf16[2,40,1280]{2,1,0:T(8,128)(2,1)}, bf16[2,40,1280]{2,1,0:T(8,128)(2,1)}, u32[]{:S(2)}, u32[]{:S(2)}) collective-permute-start(bf16[2,40,1280]{2,1,0:T(8,128)(2,1)} %get-tuple-element.70), channel_id=1, source_target_pairs={{0,10},{2,8},{4,14},{6,12},{8,2},{10,0},{12,6},{14,4},{16,26},{18,... | collective-permute-start | bytes 614408 | tf_op jit(solution)/shard_map/ppermute | solution.py:511
  339.8 24.2 %collective-permute-start.20 = (bf16[2,40,1280]{2,1,0:T(8,128)(2,1)}, bf16[2,40,1280]{2,1,0:T(8,128)(2,1)S(1)}, u32[]{:S(2)}, u32[]{:S(2)}) collective-permute-start(bf16[2,40,1280]{2,1,0:T(8,128)(2,1)} %get-tuple-element.71), channel_id=1, source_target_pairs={{0,12},{2,14},{4,8},{6,10},{8,4},{10,6},{12,0},{14,2},{16,28},{18,... | collective-permute-start | bytes 614408 | tf_op jit(solution)/shard_map/ppermute | solution.py:511
  347.1 18.5 %collective-permute-start.21 = (bf16[2,40,1280]{2,1,0:T(8,128)(2,1)}, bf16[2,40,1280]{2,1,0:T(8,128)(2,1)S(1)}, u32[]{:S(2)}, u32[]{:S(2)}) collective-permute-start(bf16[2,40,1280]{2,1,0:T(8,128)(2,1)} %get-tuple-element.72), channel_id=1, source_target_pairs={{0,14},{2,12},{4,10},{6,8},{8,6},{10,4},{12,2},{14,0},{16,30},{18,... | collective-permute-start | bytes 614408 | tf_op jit(solution)/shard_map/ppermute | solution.py:511
  347.1 22.9 %collective-permute-start.22 = (bf16[2,40,1280]{2,1,0:T(8,128)(2,1)S(1)}, bf16[2,40,1280]{2,1,0:T(8,128)(2,1)S(1)}, u32[]{:S(2)}, u32[]{:S(2)}) collective-permute-start(bf16[2,40,1280]{2,1,0:T(8,128)(2,1)S(1)} %copy-done.30), channel_id=1, source_target_pairs={{0,16},{2,18},{4,20},{6,22},{8,24},{10,26},{12,28},{14,30},{16,0},... | collective-permute-start | bytes 614408 | tf_op jit(solution)/shard_map/ppermute | solution.py:511
  347.6 31.0 %collective-permute-start.23 = (bf16[2,40,1280]{2,1,0:T(8,128)(2,1)S(1)}, bf16[2,40,1280]{2,1,0:T(8,128)(2,1)S(1)}, u32[]{:S(2)}, u32[]{:S(2)}) collective-permute-start(bf16[2,40,1280]{2,1,0:T(8,128)(2,1)S(1)} %copy-done.27), channel_id=1, source_target_pairs={{0,18},{2,16},{4,22},{6,20},{8,26},{10,24},{12,30},{14,28},{16,2},... | collective-permute-start | bytes 614408 | tf_op jit(solution)/shard_map/ppermute | solution.py:511
  362.3 19.7 %collective-permute-start.24 = (bf16[2,40,1280]{2,1,0:T(8,128)(2,1)S(1)}, bf16[2,40,1280]{2,1,0:T(8,128)(2,1)S(1)}, u32[]{:S(2)}, u32[]{:S(2)}) collective-permute-start(bf16[2,40,1280]{2,1,0:T(8,128)(2,1)S(1)} %copy-done.25), channel_id=1, source_target_pairs={{0,20},{2,22},{4,16},{6,18},{8,28},{10,30},{12,24},{14,26},{16,4},... | collective-permute-start | bytes 614408 | tf_op jit(solution)/shard_map/ppermute | solution.py:511
  364.0 43.3 %collective-permute-start.25 = (bf16[2,40,1280]{2,1,0:T(8,128)(2,1)S(1)}, bf16[2,40,1280]{2,1,0:T(8,128)(2,1)S(1)}, u32[]{:S(2)}, u32[]{:S(2)}) collective-permute-start(bf16[2,40,1280]{2,1,0:T(8,128)(2,1)S(1)} %copy-done.24), channel_id=1, source_target_pairs={{0,22},{2,20},{4,18},{6,16},{8,30},{10,28},{12,26},{14,24},{16,6},... | collective-permute-start | bytes 614408 | tf_op jit(solution)/shard_map/ppermute | solution.py:511
  365.6 41.8 %collective-permute-start.26 = (bf16[2,40,1280]{2,1,0:T(8,128)(2,1)S(1)}, bf16[2,40,1280]{2,1,0:T(8,128)(2,1)S(1)}, u32[]{:S(2)}, u32[]{:S(2)}) collective-permute-start(bf16[2,40,1280]{2,1,0:T(8,128)(2,1)S(1)} %copy-done.23), channel_id=1, source_target_pairs={{0,24},{2,26},{4,28},{6,30},{8,16},{10,18},{12,20},{14,22},{16,8},... | collective-permute-start | bytes 614408 | tf_op jit(solution)/shard_map/ppermute | solution.py:511
  370.0 37.3 %collective-permute-start.27 = (bf16[2,40,1280]{2,1,0:T(8,128)(2,1)S(1)}, bf16[2,40,1280]{2,1,0:T(8,128)(2,1)S(1)}, u32[]{:S(2)}, u32[]{:S(2)}) collective-permute-start(bf16[2,40,1280]{2,1,0:T(8,128)(2,1)S(1)} %copy-done.22), channel_id=1, source_target_pairs={{0,26},{2,24},{4,30},{6,28},{8,18},{10,16},{12,22},{14,20},{16,10}... | collective-permute-start | bytes 614408 | tf_op jit(solution)/shard_map/ppermute | solution.py:511
  378.6 28.8 %collective-permute-start.28 = (bf16[2,40,1280]{2,1,0:T(8,128)(2,1)S(1)}, bf16[2,40,1280]{2,1,0:T(8,128)(2,1)S(1)}, u32[]{:S(2)}, u32[]{:S(2)}) collective-permute-start(bf16[2,40,1280]{2,1,0:T(8,128)(2,1)S(1)} %copy-done.21), channel_id=1, source_target_pairs={{0,28},{2,30},{4,24},{6,26},{8,20},{10,22},{12,16},{14,18},{16,12}... | collective-permute-start | bytes 614408 | tf_op jit(solution)/shard_map/ppermute | solution.py:511
  382.7 24.7 %collective-permute-start.29 = (bf16[2,40,1280]{2,1,0:T(8,128)(2,1)S(1)}, bf16[2,40,1280]{2,1,0:T(8,128)(2,1)S(1)}, u32[]{:S(2)}, u32[]{:S(2)}) collective-permute-start(bf16[2,40,1280]{2,1,0:T(8,128)(2,1)S(1)} %copy-done.19), channel_id=1, source_target_pairs={{0,30},{2,28},{4,26},{6,24},{8,22},{10,20},{12,18},{14,16},{16,14}... | collective-permute-start | bytes 614408 | tf_op jit(solution)/shard_map/ppermute | solution.py:511
  (53 other events, 1422.0 us)
where the time goes:
time: 436 us; the launch traced here: 433 us
  Pallas kernels  172 us (39%)
  waiting for transfers between devices  122 us (28%)
  starting transfers between devices  81.1 us (19%)
  local copies, waits for them, and re-layouts  31.1 us (7%)
  other arithmetic  20.3 us (5%)
  matrix products  5.53 us (1%)
    ppermute x30, waiting for transfers between devices, exchange(): pieces.append(lax.ppermute(x[r], axes, pairs))  117 us
    pallas_call x2, Pallas kernels, fourier(): pl.pallas_call(functools.partial(fourier_kernel, first=first, sources=gro...  82.3 us
    ppermute x30, starting transfers between devices, exchange(): pieces.append(lax.ppermute(x[r], axes, pairs))  67.4 us
    pallas_call x2, Pallas kernels, analyse(): pl.pallas_call(functools.partial(analysis_kernel, slots=slots, sources=gr...  48.3 us
    pallas_call x2, Pallas kernels, synth(): pl.pallas_call(functools.partial(synth_kernel, slots=slots, split_up=spli...  41 us
    all_to_all x2, starting transfers between devices, exchange(): return lax.all_to_all(x, axes, split_axis=0, concat_axis=0, tiled=True)  12.1 us
    unnamed x106, local copies, waits for them, and re-layouts  9.5 us
  transfers between devices with their start and end apart: 33, of which 6 were waited for; matrix products, arithmetic and copies ran while one was open for 12% of the time, Pallas kernels for 29%

commit v1 on v0

--- a/solution.py
+++ b/solution.py
@@ -505,10 +505,11 @@
 
     def exchange(x, split_up):
         if split_up:
-            pieces = [x[0]]
-            for r in range(1, groups):
+            middle_bit = lax.axis_size("blk") // 2
+            pieces = list(x)
+            for r in sorted(range(1, groups), key=lambda r: (not r & middle_bit, r)):
                 pairs = [(i, i ^ r) for i in range(groups)]
-                pieces.append(lax.ppermute(x[r], axes, pairs))
+                pieces[r] = lax.ppermute(x[r], axes, pairs)
             return pieces
         return lax.all_to_all(x, axes, split_axis=0, concat_axis=0, tiled=True)
 
@@ -529,7 +530,14 @@
     tables = half_tables(order_slots, lon_count)
 
     split_up = [q % 2 == 1 for q in range(chunks)]
-    received = [exchange(synth(q, split_up[q]), split_up[q]) for q in range(chunks)]
+    received = []
+    for q in range(chunks):
+        spectra = synth(q, split_up[q])
+        if split_up[q]:
+            spectra, tables, w_low, w_high = lax.optimization_barrier(
+                (spectra, tables, w_low, w_high)
+            )
+        received.append(exchange(spectra, split_up[q]))
     old, held = None, None
     returned = []
     for q in range(chunks):

time: 436 us -> 441 us (1.011)
  waiting for transfers between devices: 122 us -> 115 us
  local copies, waits for them, and re-layouts: 31.1 us -> 37.5 us
  starting transfers between devices: 81.1 us -> 86.3 us
    optimization_barrier x0 -> x2, local copies, waits for them, and re-layouts: none -> 7.73 us  [fast_body(): lax.optimization_barrier((spectra, tables, w_low, w_high))]
    ppermute x30, waiting for transfers between devices: 117 us -> 110 us  [exchange(): pieces[r] = lax.ppermute(x[r], axes, pairs)]
    rev x1, local copies, waits for them, and re-layouts: 0.47 us -> 6.29 us  [fast_body(): turned = jnp.where(south, jnp.flip(weight, 0), weight)]
    ppermute x30, starting transfers between devices: 67.4 us -> 72.5 us  [exchange(): pieces[r] = lax.ppermute(x[r], axes, pairs)]
    unnamed x106 -> x100, local copies, waits for them, and re-layouts: 9.5 us -> 8.13 us
  transfers between devices with their start and end apart: 33 -> 33, of which waited for: 6 -> 6; matrix products, arithmetic and copies ran while one was open for 12% -> 14% of each run, Pallas kernels for 29% -> 29%
where the time goes in v1:
time: 441 us; the launch traced here: 438 us
  Pallas kernels  171 us (39%)
  waiting for transfers between devices  115 us (26%)
  starting transfers between devices  86.3 us (20%)
  local copies, waits for them, and re-layouts  37.5 us (9%)
  other arithmetic  20.8 us (5%)
  matrix products  5.53 us (1%)
    ppermute x30, waiting for transfers between devices, exchange(): pieces[r] = lax.ppermute(x[r], axes, pairs)  110 us
    pallas_call x2, Pallas kernels, fourier(): pl.pallas_call(functools.partial(fourier_kernel, first=first, sources=gro...  82.2 us
    ppermute x30, starting transfers between devices, exchange(): pieces[r] = lax.ppermute(x[r], axes, pairs)  72.5 us
    pallas_call x2, Pallas kernels, analyse(): pl.pallas_call(functools.partial(analysis_kernel, slots=slots, sources=gr...  48.2 us
    pallas_call x2, Pallas kernels, synth(): pl.pallas_call(functools.partial(synth_kernel, slots=slots, split_up=spli...  40.8 us
    all_to_all x2, starting transfers between devices, exchange(): return lax.all_to_all(x, axes, split_axis=0, concat_axis=0, tiled=True)  12.2 us
  transfers between devices with their start and end apart: 33, of which 6 were waited for; matrix products, arithmetic and copies ran while one was open for 14% of the time, Pallas kernels for 29%

profile of v1, /device:TPU:0, one launch (start us, length us, event | category | flops | bytes accessed | tf_op | source)
XLA Modules:
  0.0 438.2 jit_solution(6116252306308772348)
XLA Ops:
  1.9 20.3 %synth.3 = bf16[16,2,40,1280]{3,2,1,0:T(8,128)(2,1)} custom-call(s32[640]{0:T(1024)} %orders_ref.7, s32[1]{0:T(128)} %bitcast.me_ref, bf16[32,2,40,640]{3,2,1,0:T(8,128)(2,1)} %x_ref.3, f32[1,640]{1,0:T(1,128)} %broadcast_in_dim.11.root_ref, bf16[320,2,40,1280]{3,2,1,0:T(8,128)(2,1)} %bitcast.41), custom_call_target="tpu_custom_call" | custom-call | flops 32768000000 | bytes 32768000 | tf_op jit(solution)/shard_map/synth/pallas_call | solution.py:403
  22.2 7.6 %all-to-all-start = ((bf16[16,2,40,1280]{3,2,1,0:T(8,128)(2,1)}), bf16[16,2,40,1280]{3,2,1,0:T(8,128)(2,1)}, u32[]{:S(2)}, u32[]{:S(2)}) async-start(bf16[16,2,40,1280]{3,2,1,0:T(8,128)(2,1)} %synth.3), calls=%async_computation | async-start | bytes 6553600 | tf_op jit(solution)/shard_map/all_to_all | solution.py:514
  32.2 6.3 %rev.12 = f32[80,2560]{1,0:T(8,128)} reverse(f32[80,2560]{1,0:T(8,128)S(1)} %copy-done.2), dimensions={0} | reverse | bytes 1638400 | tf_op jit(solution)/shard_map/jit(_flip)/rev | solution.py:522
  38.5 3.8 multiply_add_fusion
  49.6 4.6 %copy.19 = f32[640,1280]{1,0:T(8,128)} copy(f32[640,1280]{0,1:T(8,128)} %bitcast.30) | data formatting | bytes 6553600 | tf_op jit(solution)/shard_map/add | solution.py:340
  54.2 3.0 copy.17
  57.2 4.4 reverse
  61.9 3.6 subtract_convert_fusion
  66.1 3.1 pad_maximum_fusion.2
  69.2 20.5 %synth.2 = (bf16[2,40,1280]{2,1,0:T(8,128)(2,1)}, bf16[2,40,1280]{2,1,0:T(8,128)(2,1)}, bf16[2,40,1280]{2,1,0:T(8,128)(2,1)}, bf16[2,40,1280]{2,1,0:T(8,128)(2,1...) custom-call(s32[640]{0:T(1024)} %orders_ref.7, ...), custom_call_target="tpu_custom_call" | custom-call | flops 32768000000 | bytes 32768000 | tf_op jit(solution)/shard_map/synth/pallas_call | solution.py:403
  100.2 4.6 %copy.24.refs_4_ = f32[1280,640]{1,0:T(8,128)} copy(f32[1280,640]{0,1:T(8,128)} %bitcast.34) | data formatting | bytes 6553600 | tf_op jit(solution)/shard_map/optimization_barrier | solution.py:537
  104.7 3.2 copy.25.refs_5_
  109.6 2.7 collective-permute-start.13
  112.3 10.0 %collective-permute-done.1.refs_12_ = bf16[2,40,1280]{2,1,0:T(8,128)(2,1)} collective-permute-done((bf16[2,40,1280]{2,1,0:T(8,128)(2,1)}, bf16[2,40,1280]{2,1,0:T(8,128)(2,1)}, u32[]{:S(2)}, u32[]{:S(2)}) %collective-permute-start.1) | collective-permute-done | bytes 204832 | tf_op jit(solution)/shard_map/ppermute | solution.py:512
  126.9 9.5 %collective-permute-start.4 = (bf16[2,40,1280]{2,1,0:T(8,128)(2,1)}, bf16[2,40,1280]{2,1,0:T(8,128)(2,1)S(1)}, u32[]{:S(2)}, u32[]{:S(2)}) collective-permute-start(bf16[2,40,1280]{2,1,0:T(8,128)(2,1)} %get-tuple-element.98), channel_id=1, source_target_pairs={{0,10},{2,8},{4,14},{6,12},{8,2},{10,0},{12,6},{14,4},{16,26},{18,... | collective-permute-start | bytes 614408 | tf_op jit(solution)/shard_map/ppermute | solution.py:512
  136.4 40.4 %fourier.2 = (bf16[16,2,40,1280]{3,2,1,0:T(8,128)(2,1)}, f32[1280,640]{1,0:T(8,128)}, f32[1280,640]{1,0:T(8,128)}) custom-call(s32[1]{0:T(128)} %bitcast.me_ref, bf16[5,512,640]{2,1,0:T(8,128)(2,1)} %pad_maximum_fusion.refs_0_, bf16[5,512,640]{2,1,0:T(8,128)(2,1)} %pad_maximum_fusion.1.refs_1_, bf16[1280,1280]{1,0:T(8,128)(2,1)} %get-tuple-element.87.refs_2_, ...), custom_call_target="tpu_custom_call" | custom-call | flops 41943040000 | bytes 26214400 | tf_op jit(solution)/shard_map/fourier/pallas_call | solution.py:466
  176.8 4.6 %all-to-all-start.1 = ((bf16[16,2,40,1280]{3,2,1,0:T(8,128)(2,1)}), bf16[16,2,40,1280]{3,2,1,0:T(8,128)(2,1)}, u32[]{:S(2)}, u32[]{:S(2)}) async-start(bf16[16,2,40,1280]{3,2,1,0:T(8,128)(2,1)} %get-tuple-element.125), calls=%async_computation.1 | async-start | bytes 6553600 | tf_op jit(solution)/shard_map/all_to_all | solution.py:514
  187.2 3.9 collective-permute-start.9
  191.8 82.4 %collective-permute-done.5.refs_16_ = bf16[2,40,1280]{2,1,0:T(8,128)(2,1)S(1)} collective-permute-done((bf16[2,40,1280]{2,1,0:T(8,128)(2,1)S(1)}, bf16[2,40,1280]{2,1,0:T(8,128)(2,1)S(1)}, u32[]{:S(2)}, u32[]{:S(2)}) %collective-permute-start.5) | collective-permute-done | bytes 204832 | tf_op jit(solution)/shard_map/ppermute | solution.py:512
  274.3 10.4 %collective-permute-done.9.refs_20_ = bf16[2,40,1280]{2,1,0:T(8,128)(2,1)S(1)} collective-permute-done((bf16[2,40,1280]{2,1,0:T(8,128)(2,1)S(1)}, bf16[2,40,1280]{2,1,0:T(8,128)(2,1)S(1)}, u32[]{:S(2)}, u32[]{:S(2)}) %collective-permute-start.9) | collective-permute-done | bytes 204832 | tf_op jit(solution)/shard_map/ppermute | solution.py:512
  285.3 41.8 %fourier.3 = (bf16[2,40,1280]{2,1,0:T(8,128)(2,1)}, bf16[2,40,1280]{2,1,0:T(8,128)(2,1)}, bf16[2,40,1280]{2,1,0:T(8,128)(2,1)}, bf16[2,40,1280]{2,1,0:T(8,128)(2...) custom-call(s32[1]{0:T(128)} %bitcast.me_ref, ...), custom_call_target="tpu_custom_call", output_to_operand_aliasing={{16}: (9, {}), {17}: (10, {})} | custom-call | flops 41943040000 | bytes 26214400 | tf_op jit(solution)/shard_map/fourier/pallas_call | solution.py:466
  327.2 3.8 fusion.11
  334.5 2.7 collective-permute-start.16
  338.9 4.9 %collective-permute-done.30 = f32[80,1280]{1,0:T(8,128)S(1)} collective-permute-done((f32[80,1280]{1,0:T(8,128)S(1)}, f32[80,1280]{1,0:T(8,128)S(1)}, u32[]{:S(2)}, u32[]{:S(2)}) %collective-permute-start.30) | collective-permute-done | bytes 409632 | tf_op jit(solution)/shard_map/ppermute | solution.py:570
  345.1 3.0 collective-permute-start.20
  348.1 4.3 collective-permute-done.16.refs_2_
  352.9 14.7 %collective-permute-start.23 = (bf16[2,40,1280]{2,1,0:T(8,128)(2,1)S(1)}, bf16[2,40,1280]{2,1,0:T(8,128)(2,1)S(1)}, u32[]{:S(2)}, u32[]{:S(2)}) collective-permute-start(bf16[2,40,1280]{2,1,0:T(8,128)(2,1)S(1)} %copy-done.24), channel_id=1, source_target_pairs={{0,18},{2,16},{4,22},{6,20},{8,26},{10,24},{12,30},{14,28},{16,2},... | collective-permute-start | bytes 614408 | tf_op jit(solution)/shard_map/ppermute | solution.py:512
  370.9 4.5 %collective-permute-start.26 = (bf16[2,40,1280]{2,1,0:T(8,128)(2,1)S(1)}, bf16[2,40,1280]{2,1,0:T(8,128)(2,1)S(1)}, u32[]{:S(2)}, u32[]{:S(2)}) collective-permute-start(bf16[2,40,1280]{2,1,0:T(8,128)(2,1)S(1)} %copy-done.15), channel_id=1, source_target_pairs={{0,24},{2,26},{4,28},{6,30},{8,16},{10,18},{12,20},{14,22},{16,8},... | collective-permute-start | bytes 614408 | tf_op jit(solution)/shard_map/ppermute | solution.py:512
  375.4 8.5 %collective-permute-start.27 = (bf16[2,40,1280]{2,1,0:T(8,128)(2,1)S(1)}, bf16[2,40,1280]{2,1,0:T(8,128)(2,1)S(1)}, u32[]{:S(2)}, u32[]{:S(2)}) collective-permute-start(bf16[2,40,1280]{2,1,0:T(8,128)(2,1)S(1)} %copy-done.14), channel_id=1, source_target_pairs={{0,26},{2,24},{4,30},{6,28},{8,18},{10,16},{12,22},{14,20},{16,10}... | collective-permute-start | bytes 614408 | tf_op jit(solution)/shard_map/ppermute | solution.py:512
  384.2 3.2 collective-permute-done.24.refs_10_
  388.8 23.8 %analyse.2.refs_16_ = f32[32,2,40,640]{3,2,1,0:T(8,128)} custom-call(s32[640]{0:T(1024)} %orders_ref.7, s32[1]{0:T(128)} %bitcast.me_ref, f32[1,640]{1,0:T(1,128)} %broadcast_in_dim.11.root_ref, bf16[320,2,40,1280]{3,2,1,0:T(8,128)(2,1)} %bitcast.43, bf16[16,2,40,1280]{3,2,1,0:T(8,128)(2,1)} %all-to-all-done.1.refs_0_), custom_call_target="tpu_custom_call" | custom-call | flops 32768000000 | bytes 32768000 | tf_op jit(solution)/shard_map/analyse/pallas_call | solution.py:428
  413.6 24.4 %analyse.3 = f32[32,2,40,640]{3,2,1,0:T(8,128)} custom-call(s32[640]{0:T(1024)} %orders_ref.7, s32[1]{0:T(128)} %bitcast.me_ref, f32[1,640]{1,0:T(1,128)} %broadcast_in_dim.11.root_ref, bf16[320,2,40,1280]{3,2,1,0:T(8,128)(2,1)} %bitcast.44, bf16[2,40,1280]{2,1,0:T(8,128)(2,1)} %get-tuple-element.109.refs_0_, ...), custom_call_target="tpu_custom_call", output_to_operand_aliasing={{}: (20, {})} | custom-call | flops 32768000000 | bytes 32768000 | tf_op jit(solution)/shard_map/analyse/pallas_call | solution.py:428
  (183 shorter events, 48.4 us)
Async XLA Ops:
  22.2 114.2 %all-to-all-start = ((bf16[16,2,40,1280]{3,2,1,0:T(8,128)(2,1)}), bf16[16,2,40,1280]{3,2,1,0:T(8,128)(2,1)}, u32[]{:S(2)}, u32[]{:S(2)}) async-start(bf16[16,2,40,1280]{3,2,1,0:T(8,128)(2,1)} %synth.3), calls=%async_computation | async-start | bytes 6553600 | tf_op jit(solution)/shard_map/all_to_all | solution.py:514
  92.7 16.9 %collective-permute-start = (bf16[2,40,1280]{2,1,0:T(8,128)(2,1)}, bf16[2,40,1280]{2,1,0:T(8,128)(2,1)S(1)}, u32[]{:S(2)}, u32[]{:S(2)}) collective-permute-start(bf16[2,40,1280]{2,1,0:T(8,128)(2,1)} %get-tuple-element.94), channel_id=1, source_target_pairs={{0,2},{2,0},{4,6},{6,4},{8,10},{10,8},{12,14},{14,12},{16,18},{18,... | collective-permute-start | bytes 614408 | tf_op jit(solution)/shard_map/ppermute | solution.py:512
  94.6 27.8 %collective-permute-start.1 = (bf16[2,40,1280]{2,1,0:T(8,128)(2,1)}, bf16[2,40,1280]{2,1,0:T(8,128)(2,1)}, u32[]{:S(2)}, u32[]{:S(2)}) collective-permute-start(bf16[2,40,1280]{2,1,0:T(8,128)(2,1)} %get-tuple-element.95), channel_id=1, source_target_pairs={{0,4},{2,6},{4,0},{6,2},{8,12},{10,14},{12,8},{14,10},{16,20},{18,... | collective-permute-start | bytes 614408 | tf_op jit(solution)/shard_map/ppermute | solution.py:512
  96.9 26.8 %collective-permute-start.10 = (bf16[2,40,1280]{2,1,0:T(8,128)(2,1)}, bf16[2,40,1280]{2,1,0:T(8,128)(2,1)}, u32[]{:S(2)}, u32[]{:S(2)}) collective-permute-start(bf16[2,40,1280]{2,1,0:T(8,128)(2,1)} %get-tuple-element.104), channel_id=1, source_target_pairs={{0,22},{2,20},{4,18},{6,16},{8,30},{10,28},{12,26},{14,24},{16,6},... | collective-permute-start | bytes 614408 | tf_op jit(solution)/shard_map/ppermute | solution.py:512
  98.4 27.3 %collective-permute-start.11 = (bf16[2,40,1280]{2,1,0:T(8,128)(2,1)}, bf16[2,40,1280]{2,1,0:T(8,128)(2,1)}, u32[]{:S(2)}, u32[]{:S(2)}) collective-permute-start(bf16[2,40,1280]{2,1,0:T(8,128)(2,1)} %get-tuple-element.105), channel_id=1, source_target_pairs={{0,24},{2,26},{4,28},{6,30},{8,16},{10,18},{12,20},{14,22},{16,8},... | collective-permute-start | bytes 614408 | tf_op jit(solution)/shard_map/ppermute | solution.py:512
  98.4 28.5 %collective-permute-start.12 = (bf16[2,40,1280]{2,1,0:T(8,128)(2,1)}, bf16[2,40,1280]{2,1,0:T(8,128)(2,1)}, u32[]{:S(2)}, u32[]{:S(2)}) collective-permute-start(bf16[2,40,1280]{2,1,0:T(8,128)(2,1)} %get-tuple-element.106), channel_id=1, source_target_pairs={{0,26},{2,24},{4,30},{6,28},{8,18},{10,16},{12,22},{14,20},{16,10}... | collective-permute-start | bytes 614408 | tf_op jit(solution)/shard_map/ppermute | solution.py:512
  109.6 71.9 %collective-permute-start.13 = (bf16[2,40,1280]{2,1,0:T(8,128)(2,1)}, bf16[2,40,1280]{2,1,0:T(8,128)(2,1)S(1)}, u32[]{:S(2)}, u32[]{:S(2)}) collective-permute-start(bf16[2,40,1280]{2,1,0:T(8,128)(2,1)} %get-tuple-element.107), channel_id=1, source_target_pairs={{0,28},{2,30},{4,24},{6,26},{8,20},{10,22},{12,16},{14,18},{16,12}... | collective-permute-start | bytes 614408 | tf_op jit(solution)/shard_map/ppermute | solution.py:512
  122.3 61.7 %collective-permute-start.14 = (bf16[2,40,1280]{2,1,0:T(8,128)(2,1)}, bf16[2,40,1280]{2,1,0:T(8,128)(2,1)S(1)}, u32[]{:S(2)}, u32[]{:S(2)}) collective-permute-start(bf16[2,40,1280]{2,1,0:T(8,128)(2,1)} %get-tuple-element.108), channel_id=1, source_target_pairs={{0,30},{2,28},{4,26},{6,24},{8,22},{10,20},{12,18},{14,16},{16,14}... | collective-permute-start | bytes 614408 | tf_op jit(solution)/shard_map/ppermute | solution.py:512
  123.8 61.7 %collective-permute-start.2 = (bf16[2,40,1280]{2,1,0:T(8,128)(2,1)}, bf16[2,40,1280]{2,1,0:T(8,128)(2,1)S(1)}, u32[]{:S(2)}, u32[]{:S(2)}) collective-permute-start(bf16[2,40,1280]{2,1,0:T(8,128)(2,1)} %get-tuple-element.96), channel_id=1, source_target_pairs={{0,6},{2,4},{4,2},{6,0},{8,14},{10,12},{12,10},{14,8},{16,22},{18,... | collective-permute-start | bytes 614408 | tf_op jit(solution)/shard_map/ppermute | solution.py:512
  125.6 61.4 %collective-permute-start.3 = (bf16[2,40,1280]{2,1,0:T(8,128)(2,1)}, bf16[2,40,1280]{2,1,0:T(8,128)(2,1)S(1)}, u32[]{:S(2)}, u32[]{:S(2)}) collective-permute-start(bf16[2,40,1280]{2,1,0:T(8,128)(2,1)} %get-tuple-element.97), channel_id=1, source_target_pairs={{0,8},{2,10},{4,12},{6,14},{8,0},{10,2},{12,4},{14,6},{16,24},{18,... | collective-permute-start | bytes 614408 | tf_op jit(solution)/shard_map/ppermute | solution.py:512
  126.9 60.3 %collective-permute-start.4 = (bf16[2,40,1280]{2,1,0:T(8,128)(2,1)}, bf16[2,40,1280]{2,1,0:T(8,128)(2,1)S(1)}, u32[]{:S(2)}, u32[]{:S(2)}) collective-permute-start(bf16[2,40,1280]{2,1,0:T(8,128)(2,1)} %get-tuple-element.98), channel_id=1, source_target_pairs={{0,10},{2,8},{4,14},{6,12},{8,2},{10,0},{12,6},{14,4},{16,26},{18,... | collective-permute-start | bytes 614408 | tf_op jit(solution)/shard_map/ppermute | solution.py:512
  176.8 211.9 %all-to-all-start.1 = ((bf16[16,2,40,1280]{3,2,1,0:T(8,128)(2,1)}), bf16[16,2,40,1280]{3,2,1,0:T(8,128)(2,1)}, u32[]{:S(2)}, u32[]{:S(2)}) async-start(bf16[16,2,40,1280]{3,2,1,0:T(8,128)(2,1)} %get-tuple-element.125), calls=%async_computation.1 | async-start | bytes 6553600 | tf_op jit(solution)/shard_map/all_to_all | solution.py:514
  181.5 92.7 %collective-permute-start.5 = (bf16[2,40,1280]{2,1,0:T(8,128)(2,1)S(1)}, bf16[2,40,1280]{2,1,0:T(8,128)(2,1)S(1)}, u32[]{:S(2)}, u32[]{:S(2)}) collective-permute-start(bf16[2,40,1280]{2,1,0:T(8,128)(2,1)S(1)} %copy-done.22), channel_id=1, source_target_pairs={{0,12},{2,14},{4,8},{6,10},{8,4},{10,6},{12,0},{14,2},{16,28},{18,... | collective-permute-start | bytes 614408 | tf_op jit(solution)/shard_map/ppermute | solution.py:512
  184.0 90.2 %collective-permute-start.6 = (bf16[2,40,1280]{2,1,0:T(8,128)(2,1)S(1)}, bf16[2,40,1280]{2,1,0:T(8,128)(2,1)S(1)}, u32[]{:S(2)}, u32[]{:S(2)}) collective-permute-start(bf16[2,40,1280]{2,1,0:T(8,128)(2,1)S(1)} %copy-done.20), channel_id=1, source_target_pairs={{0,14},{2,12},{4,10},{6,8},{8,6},{10,4},{12,2},{14,0},{16,30},{18,... | collective-permute-start | bytes 614408 | tf_op jit(solution)/shard_map/ppermute | solution.py:512
  185.5 88.7 %collective-permute-start.7 = (bf16[2,40,1280]{2,1,0:T(8,128)(2,1)S(1)}, bf16[2,40,1280]{2,1,0:T(8,128)(2,1)S(1)}, u32[]{:S(2)}, u32[]{:S(2)}) collective-permute-start(bf16[2,40,1280]{2,1,0:T(8,128)(2,1)S(1)} %copy-done.19), channel_id=1, source_target_pairs={{0,16},{2,18},{4,20},{6,22},{8,24},{10,26},{12,28},{14,30},{16,0},... | collective-permute-start | bytes 614408 | tf_op jit(solution)/shard_map/ppermute | solution.py:512
  187.1 87.2 %collective-permute-start.8 = (bf16[2,40,1280]{2,1,0:T(8,128)(2,1)S(1)}, bf16[2,40,1280]{2,1,0:T(8,128)(2,1)S(1)}, u32[]{:S(2)}, u32[]{:S(2)}) collective-permute-start(bf16[2,40,1280]{2,1,0:T(8,128)(2,1)S(1)} %copy-done.18), channel_id=1, source_target_pairs={{0,18},{2,16},{4,22},{6,20},{8,26},{10,24},{12,30},{14,28},{16,2},... | collective-permute-start | bytes 614408 | tf_op jit(solution)/shard_map/ppermute | solution.py:512
  187.2 97.4 %collective-permute-start.9 = (bf16[2,40,1280]{2,1,0:T(8,128)(2,1)S(1)}, bf16[2,40,1280]{2,1,0:T(8,128)(2,1)S(1)}, u32[]{:S(2)}, u32[]{:S(2)}) collective-permute-start(bf16[2,40,1280]{2,1,0:T(8,128)(2,1)S(1)} %copy-done.17), channel_id=1, source_target_pairs={{0,20},{2,22},{4,16},{6,18},{8,28},{10,30},{12,24},{14,26},{16,4},... | collective-permute-start | bytes 614408 | tf_op jit(solution)/shard_map/ppermute | solution.py:512
  332.8 11.0 %collective-permute-start.30 = (f32[80,1280]{1,0:T(8,128)S(1)}, f32[80,1280]{1,0:T(8,128)S(1)}, u32[]{:S(2)}, u32[]{:S(2)}) collective-permute-start(f32[80,1280]{1,0:T(8,128)S(1)} %get-tuple-element.146), channel_id=1, source_target_pairs={{0,1},{1,0},{2,3},{3,2},{4,5},{5,4},{6,7},{7,6},{8,9},{9,8},{10,11... | collective-permute-start | bytes 1228808 | tf_op jit(solution)/shard_map/ppermute | solution.py:570
  334.5 17.9 %collective-permute-start.16 = (bf16[2,40,1280]{2,1,0:T(8,128)(2,1)}, bf16[2,40,1280]{2,1,0:T(8,128)(2,1)S(1)}, u32[]{:S(2)}, u32[]{:S(2)}) collective-permute-start(bf16[2,40,1280]{2,1,0:T(8,128)(2,1)} %get-tuple-element.111), channel_id=1, source_target_pairs={{0,4},{2,6},{4,0},{6,2},{8,12},{10,14},{12,8},{14,10},{16,20},{18,... | collective-permute-start | bytes 614408 | tf_op jit(solution)/shard_map/ppermute | solution.py:512
  337.2 15.2 %collective-permute-start.17 = (bf16[2,40,1280]{2,1,0:T(8,128)(2,1)}, bf16[2,40,1280]{2,1,0:T(8,128)(2,1)S(1)}, u32[]{:S(2)}, u32[]{:S(2)}) collective-permute-start(bf16[2,40,1280]{2,1,0:T(8,128)(2,1)} %get-tuple-element.112), channel_id=1, source_target_pairs={{0,6},{2,4},{4,2},{6,0},{8,14},{10,12},{12,10},{14,8},{16,22},{18,... | collective-permute-start | bytes 614408 | tf_op jit(solution)/shard_map/ppermute | solution.py:512
  338.9 14.0 %collective-permute-start.18 = (bf16[2,40,1280]{2,1,0:T(8,128)(2,1)}, bf16[2,40,1280]{2,1,0:T(8,128)(2,1)}, u32[]{:S(2)}, u32[]{:S(2)}) collective-permute-start(bf16[2,40,1280]{2,1,0:T(8,128)(2,1)} %get-tuple-element.113), channel_id=1, source_target_pairs={{0,8},{2,10},{4,12},{6,14},{8,0},{10,2},{12,4},{14,6},{16,24},{18,... | collective-permute-start | bytes 614408 | tf_op jit(solution)/shard_map/ppermute | solution.py:512
  343.8 23.8 %collective-permute-start.19 = (bf16[2,40,1280]{2,1,0:T(8,128)(2,1)}, bf16[2,40,1280]{2,1,0:T(8,128)(2,1)}, u32[]{:S(2)}, u32[]{:S(2)}) collective-permute-start(bf16[2,40,1280]{2,1,0:T(8,128)(2,1)} %get-tuple-element.114), channel_id=1, source_target_pairs={{0,10},{2,8},{4,14},{6,12},{8,2},{10,0},{12,6},{14,4},{16,26},{18,... | collective-permute-start | bytes 614408 | tf_op jit(solution)/shard_map/ppermute | solution.py:512
  345.1 24.2 %collective-permute-start.20 = (bf16[2,40,1280]{2,1,0:T(8,128)(2,1)}, bf16[2,40,1280]{2,1,0:T(8,128)(2,1)S(1)}, u32[]{:S(2)}, u32[]{:S(2)}) collective-permute-start(bf16[2,40,1280]{2,1,0:T(8,128)(2,1)} %get-tuple-element.115), channel_id=1, source_target_pairs={{0,12},{2,14},{4,8},{6,10},{8,4},{10,6},{12,0},{14,2},{16,28},{18,... | collective-permute-start | bytes 614408 | tf_op jit(solution)/shard_map/ppermute | solution.py:512
  352.4 18.5 %collective-permute-start.21 = (bf16[2,40,1280]{2,1,0:T(8,128)(2,1)}, bf16[2,40,1280]{2,1,0:T(8,128)(2,1)S(1)}, u32[]{:S(2)}, u32[]{:S(2)}) collective-permute-start(bf16[2,40,1280]{2,1,0:T(8,128)(2,1)} %get-tuple-element.116), channel_id=1, source_target_pairs={{0,14},{2,12},{4,10},{6,8},{8,6},{10,4},{12,2},{14,0},{16,30},{18,... | collective-permute-start | bytes 614408 | tf_op jit(solution)/shard_map/ppermute | solution.py:512
  352.5 22.9 %collective-permute-start.22 = (bf16[2,40,1280]{2,1,0:T(8,128)(2,1)S(1)}, bf16[2,40,1280]{2,1,0:T(8,128)(2,1)S(1)}, u32[]{:S(2)}, u32[]{:S(2)}) collective-permute-start(bf16[2,40,1280]{2,1,0:T(8,128)(2,1)S(1)} %copy-done.27), channel_id=1, source_target_pairs={{0,16},{2,18},{4,20},{6,22},{8,24},{10,26},{12,28},{14,30},{16,0},... | collective-permute-start | bytes 614408 | tf_op jit(solution)/shard_map/ppermute | solution.py:512
  352.9 31.0 %collective-permute-start.23 = (bf16[2,40,1280]{2,1,0:T(8,128)(2,1)S(1)}, bf16[2,40,1280]{2,1,0:T(8,128)(2,1)S(1)}, u32[]{:S(2)}, u32[]{:S(2)}) collective-permute-start(bf16[2,40,1280]{2,1,0:T(8,128)(2,1)S(1)} %copy-done.24), channel_id=1, source_target_pairs={{0,18},{2,16},{4,22},{6,20},{8,26},{10,24},{12,30},{14,28},{16,2},... | collective-permute-start | bytes 614408 | tf_op jit(solution)/shard_map/ppermute | solution.py:512
  367.7 19.7 %collective-permute-start.24 = (bf16[2,40,1280]{2,1,0:T(8,128)(2,1)S(1)}, bf16[2,40,1280]{2,1,0:T(8,128)(2,1)S(1)}, u32[]{:S(2)}, u32[]{:S(2)}) collective-permute-start(bf16[2,40,1280]{2,1,0:T(8,128)(2,1)S(1)} %copy-done.21), channel_id=1, source_target_pairs={{0,20},{2,22},{4,16},{6,18},{8,28},{10,30},{12,24},{14,26},{16,4},... | collective-permute-start | bytes 614408 | tf_op jit(solution)/shard_map/ppermute | solution.py:512
  369.4 43.3 %collective-permute-start.25 = (bf16[2,40,1280]{2,1,0:T(8,128)(2,1)S(1)}, bf16[2,40,1280]{2,1,0:T(8,128)(2,1)S(1)}, u32[]{:S(2)}, u32[]{:S(2)}) collective-permute-start(bf16[2,40,1280]{2,1,0:T(8,128)(2,1)S(1)} %copy-done.16), channel_id=1, source_target_pairs={{0,22},{2,20},{4,18},{6,16},{8,30},{10,28},{12,26},{14,24},{16,6},... | collective-permute-start | bytes 614408 | tf_op jit(solution)/shard_map/ppermute | solution.py:512
  370.9 41.7 %collective-permute-start.26 = (bf16[2,40,1280]{2,1,0:T(8,128)(2,1)S(1)}, bf16[2,40,1280]{2,1,0:T(8,128)(2,1)S(1)}, u32[]{:S(2)}, u32[]{:S(2)}) collective-permute-start(bf16[2,40,1280]{2,1,0:T(8,128)(2,1)S(1)} %copy-done.15), channel_id=1, source_target_pairs={{0,24},{2,26},{4,28},{6,30},{8,16},{10,18},{12,20},{14,22},{16,8},... | collective-permute-start | bytes 614408 | tf_op jit(solution)/shard_map/ppermute | solution.py:512
  375.4 37.3 %collective-permute-start.27 = (bf16[2,40,1280]{2,1,0:T(8,128)(2,1)S(1)}, bf16[2,40,1280]{2,1,0:T(8,128)(2,1)S(1)}, u32[]{:S(2)}, u32[]{:S(2)}) collective-permute-start(bf16[2,40,1280]{2,1,0:T(8,128)(2,1)S(1)} %copy-done.14), channel_id=1, source_target_pairs={{0,26},{2,24},{4,30},{6,28},{8,18},{10,16},{12,22},{14,20},{16,10}... | collective-permute-start | bytes 614408 | tf_op jit(solution)/shard_map/ppermute | solution.py:512
  383.9 28.8 %collective-permute-start.28 = (bf16[2,40,1280]{2,1,0:T(8,128)(2,1)S(1)}, bf16[2,40,1280]{2,1,0:T(8,128)(2,1)S(1)}, u32[]{:S(2)}, u32[]{:S(2)}) collective-permute-start(bf16[2,40,1280]{2,1,0:T(8,128)(2,1)S(1)} %copy-done.13), channel_id=1, source_target_pairs={{0,28},{2,30},{4,24},{6,26},{8,20},{10,22},{12,16},{14,18},{16,12}... | collective-permute-start | bytes 614408 | tf_op jit(solution)/shard_map/ppermute | solution.py:512
  388.0 24.7 %collective-permute-start.29 = (bf16[2,40,1280]{2,1,0:T(8,128)(2,1)S(1)}, bf16[2,40,1280]{2,1,0:T(8,128)(2,1)S(1)}, u32[]{:S(2)}, u32[]{:S(2)}) collective-permute-start(bf16[2,40,1280]{2,1,0:T(8,128)(2,1)S(1)} %copy-done.12), channel_id=1, source_target_pairs={{0,30},{2,28},{4,26},{6,24},{8,22},{10,20},{12,18},{14,16},{16,14}... | collective-permute-start | bytes 614408 | tf_op jit(solution)/shard_map/ppermute | solution.py:512
  (51 other events, 1362.4 us)
